TPU v7x, 32 devices: a whole 2x2x4 slice. The times are simulated.
32 devices in a mesh: pb: 4 (over z), row: 4 (over y, x), col: 2 (over core).
Axes of the slice: x: 2, y: 2, z: 4, core: 2. Of those that a mesh axis runs over, the one named last changes fastest.
Arguments:
- amplitudes: bfloat16 [4, 20, 4, 9216], P('pb'), may hold values from -6 to 6
- pairs: int32 [4, 4, 2], P('pb'), may hold values from 0 to 3
- stored_k: int32 [4], replicated, may hold values from 0 to 3, each once
- orbitals: bfloat16 [4, 192, 2048], P('pb', None, ('row', 'col')), may hold values from -1.078125 to 1.078125
- valence_energy: float32 [4, 96], replicated, may hold values from -1 to 0
- conduction_energy: float32 [4, 96], replicated, may hold values from 2.5 to 3.5
- screened: bfloat16 [4, 2048, 2048], P('pb', 'row', 'col'), may hold values from -0.125 to 0.125
Outputs:
- filtered: bfloat16 [4, 20, 4, 9216], P('pb')
Inputs may be any that keep to these rules, and one draw needn't show every extreme that they name: stored_k holds every k-point exactly once; row s of orbitals belongs to k-point stored_k[s]. `pairs`: each entry is a k-point.
All inputs are finite; a program needn't handle non-finite values.
Results may differ from a plain program's by a relative error of at most 0.024.
Values may be sent and summed in bfloat16 or wider, within the bound.
A program may use at most 64 MiB of HBM per device.

v0:
```python
import jax
import jax.numpy as jnp
from jax import lax
from jax.sharding import PartitionSpec as P

CENTER = 3.0
HALF = 2.5


def on_device(amplitudes, pairs, stored_k, orbitals, valence_energy, conduction_energy, screened):
    amplitude = amplitudes[0]
    pair_list = pairs[0]
    w_tile = screened[0]
    count_v = valence_energy.shape[1]
    count_c = conduction_energy.shape[1]
    vectors, pair_count, flat_size = amplitude.shape
    points = orbitals.shape[2]
    col_width = w_tile.shape[1]
    column = lax.axis_index("col")

    def pick(shard_piece):
        pick_low = (stored_k[None, :] == pair_list[:, 0:1]).astype(jnp.bfloat16)
        pick_high = (stored_k[None, :] == pair_list[:, 1:2]).astype(jnp.bfloat16)
        low_bands = jnp.einsum(
            "pl,lbr->pbr", pick_low, shard_piece[:, :count_v], preferred_element_type=jnp.float32
        )
        high_bands = jnp.einsum(
            "pl,lbr->pbr", pick_high, shard_piece[:, count_v:], preferred_element_type=jnp.float32
        )
        return (low_bands, high_bands)

    def fetch_each():
        found = pick(lax.all_gather(orbitals, "pb", axis=0, tiled=True))
        return (found[0].astype(jnp.bfloat16), found[1].astype(jnp.bfloat16))

    low_energy = jnp.take(valence_energy, pair_list[:, 0], axis=0)
    high_energy = jnp.take(conduction_energy, pair_list[:, 1], axis=0)
    gap_grid = (high_energy[:, None, :] - low_energy[:, :, None]).reshape(pair_count, flat_size)
    gap_rows = jnp.tile(gap_grid, (vectors, 1))

    def kernel_term(current, bands):
        valence, conduction_orbital = bands
        amplitude_lattice = current.reshape(vectors, pair_count, count_v, count_c)
        inner_total_sum = jnp.einsum(
            "iomx,oxj->iomj",
            amplitude_lattice,
            conduction_orbital,
            preferred_element_type=jnp.float32,
        )
        values = jnp.sum(valence.astype(jnp.float32)[None] * inner_total_sum, axis=2)
        values = values.astype(jnp.bfloat16).reshape(vectors * pair_count, points)
        everywhere = lax.all_gather(values, ("row", "col"), axis=1, tiled=True)
        needed = lax.dynamic_slice_in_dim(everywhere, column * col_width, col_width, 1)
        partial_value = lax.dot_general(
            needed, w_tile, (((1,), (1,)), ((), ())), preferred_element_type=jnp.float32
        )
        own_sums = (
            lax.psum_scatter(
                partial_value.astype(jnp.bfloat16), "col", scatter_dimension=1, tiled=True
            )
            .astype(jnp.float32)
            .reshape(vectors, pair_count, points)
        )
        weighted_product = (valence.astype(jnp.float32)[None] * own_sums[:, :, None, :]).astype(
            jnp.bfloat16
        )
        projected = jnp.einsum(
            "kyqz,yhz->kyqh",
            weighted_product,
            conduction_orbital,
            preferred_element_type=jnp.float32,
        )
        return projected.reshape(vectors * pair_count, flat_size)

    def advance(current_rows, summed, gap_part, previous_rows, factor):
        value = (gap_part * current_rows + summed - CENTER * current_rows) / HALF
        if previous_rows is None:
            return value.astype(jnp.bfloat16)
        return (factor * value - previous_rows).astype(jnp.bfloat16)

    def finish(partial_term, current, previous, factor):
        summed = lax.psum(partial_term.astype(jnp.bfloat16), ("row", "col")).astype(jnp.float32)
        previous_full = None
        if previous is not None:
            previous_full = previous.astype(jnp.float32)
        return advance(current.astype(jnp.float32), summed, gap_rows, previous_full, factor)

    initial = amplitude.reshape(vectors * pair_count, flat_size)
    first_bands = fetch_each()
    first_term = finish(kernel_term(initial, first_bands), initial, None, 1.0)
    second_bands = fetch_each()
    second_term = finish(kernel_term(first_term, second_bands), first_term, initial, 2.0)
    return second_term.reshape(1, vectors, pair_count, flat_size)


def solution(mesh):
    return jax.shard_map(
        on_device,
        mesh=mesh,
        in_specs=(
            P("pb", None, None, None),
            P("pb", None, None),
            P(),
            P("pb", None, ("row", "col")),
            P(),
            P(),
            P("pb", "row", "col"),
        ),
        out_specs=P("pb", None, None, None),
        check_vma=False,
    )
```

profile of v0, /device:TPU:0, one launch (start us, length us, event | category | flops | bytes accessed | tf_op | source)
XLA Modules:
  0.0 231.6 jit_solution(977043757335007725)
XLA Ops:
  6.5 0.8 slice_bitcast_fusion.1
  7.4 16.6 %all_gather.10 = bf16[4,192,256]{2,1,0:T(8,128)(2,1)S(1)} all-gather(bf16[1,192,256]{2,1,0:T(8,128)(2,1)} %param.12), channel_id=1, replica_groups=mesh['pb'=4,'row'=4,'col'=2] {'pb'}, dimensions={0}, use_global_device_ids=true | all-gather | bytes 491520 | tf_op jit(solution)/shard_map/all_gather | solution.py:33
  24.0 1.0 fusion.15
  25.0 0.1 copy.59
  25.1 0.0 copy-done.1
  25.1 2.6 %reshape_reshape_squeeze.3 = bf16[20,4,96,96]{3,2,1,0:T(8,128)(2,1)} reshape(bf16[1,20,4,9216]{3,2,1,0:T(4,128)(2,1)S(1)} %copy-done.1) | data formatting | bytes 2949120 | tf_op jit(solution)/shard_map/reshape;reshape;squeeze | solution.py:43
  27.7 0.0 copy-done.5
  27.7 0.3 fusion.16
  28.0 2.8 %fusion.1 = bf16[20,4,256]{2,0,1:T(8,128)(2,1)S(1)} fusion(f32[4,96,256]{2,1,0:T(8,128)S(1)} %copy.59, bf16[20,4,96,96]{3,2,1,0:T(8,128)(2,1)} %reshape_reshape_squeeze.3, bf16[4,96,256,1]{2,0,1,3:T(4,128)(2,1)S(1)} %fusion.16), kind=kOutput, calls=%fused_computation.5 | convolution fusion | flops 381399040 | bytes 2105344 | tf_op jit(solution)/shard_map/iomx,oxj->iomj/dot_general | solution.py:44
  30.9 10.1 %all_gather.11 = bf16[80,2048]{1,0:T(8,128)(2,1)S(1)} all-gather(bf16[80,256]{1,0:T(8,128)(2,1)S(1)} %convert_element_type.92), channel_id=1, replica_groups=mesh['pb'=4,'row'=4,'col'=2] {'row','col'}, dimensions={1}, use_global_device_ids=true | all-gather | bytes 368640 | tf_op jit(solution)/shard_map/all_gather | solution.py:52
  41.0 1.1 convolution_convert_fusion.3
  42.1 0.0 reduce-scatter.3.cloned.1.call-update
  42.1 0.0 all-reduce.3.cloned.1.call-start
  42.2 1.7 reshape.48
  43.9 6.7 %reduce-scatter.3.cloned.1.call-done = bf16[80,256]{1,0:T(8,128)(2,1)} async-done(((bf16[80,512]{1,0:T(8,128)(2,1)}), bf16[80,256]{1,0:T(8,128)(2,1)}) %reduce-scatter.3.cloned.1.call-update) | async-done | bytes 40976 | tf_op jit(solution)/shard_map/reduce_scatter | solution.py:58
  50.6 0.8 reshape.49
  51.4 2.9 %convert_bitcast_fusion.1 = bf16[20,4,96,96]{2,3,0,1:T(8,128)(2,1)} fusion(f32[20,4,256]{2,0,1:T(8,128)S(1)} %copy.63, f32[4,96,256]{2,1,0:T(8,128)S(1)} %copy.59, bf16[4,96,256,1]{2,0,1,3:T(4,128)(2,1)S(1)} %copy-done.7), kind=kOutput, calls=%fused_computation.25 | convolution fusion | flops 382156800 | bytes 2146304 | tf_op jit(solution)/shard_map/kyqz,yhz->kyqh/dot_general | solution.py:67
  54.3 3.2 %copy.65 = bf16[20,4,96,96]{3,2,1,0:T(8,128)(2,1)S(1)} copy(bf16[20,4,96,96]{2,3,0,1:T(8,128)(2,1)} %convert_bitcast_fusion.1) | data formatting | bytes 2949120 | tf_op jit(solution)/shard_map/convert_element_type | solution.py:82
  57.5 0.0 copy-start.2
  57.5 0.0 copy-start.3
  57.6 3.6 %convert_element_type.97 = bf16[80,9216]{1,0:T(8,128)(2,1)} reshape(bf16[20,4,96,96]{3,2,1,0:T(8,128)(2,1)S(1)} %copy.65) | data formatting | bytes 2949120 | tf_op jit(solution)/shard_map/convert_element_type | solution.py:82
  61.1 0.0 all-reduce.3.cloned.1.call-update
  61.1 0.0 reduce-scatter.5.cloned.1.call-start
  61.2 0.6 gather_fusion.1
  61.8 0.6 gather_fusion
  62.3 0.1 broadcast_select_fusion
  62.4 0.1 broadcast_select_fusion.1
  62.5 0.1 broadcast_subtract_fusion
  62.6 0.2 sub.32
  62.8 2.3 tile.8
  65.0 4.3 %tile.9 = f32[80,9216]{1,0:T(8,128)} reshape(f32[20,4,9216]{2,1,0:T(4,128)} %tile.8) | data formatting | bytes 5898240 | tf_op jit(solution)/shard_map/tile | solution.py:39
  69.3 51.5 %all-reduce.3.cloned.1.call-done = bf16[80,9216]{1,0:T(8,128)(2,1)} async-done(((bf16[80,9216]{1,0:T(8,128)(2,1)}), bf16[80,9216]{1,0:T(8,128)(2,1)}) %all-reduce.3.cloned.1.call-update) | async-done | bytes 1474576 | tf_op jit(solution)/shard_map/psum | solution.py:82
  120.8 3.8 %multiply_convert_fusion.4 = bf16[80,9216]{1,0:T(8,128)(2,1)S(1)} fusion(f32[80,9216]{1,0:T(8,128)} %reshape.48, bf16[80,9216]{1,0:T(8,128)(2,1)} %all-reduce.3.cloned.1.call-done, f32[80,9216]{1,0:T(8,128)} %tile.9), kind=kLoop, calls=%fused_computation.21 | loop fusion | flops 5160960 | bytes 8847360 | tf_op jit(solution)/shard_map/convert_element_type | solution.py:78
  124.6 2.9 %reshape.46 = bf16[20,4,96,96]{3,2,1,0:T(8,128)(2,1)} reshape(bf16[80,9216]{1,0:T(8,128)(2,1)S(1)} %multiply_convert_fusion.4) | data formatting | bytes 2949120 | tf_op jit(solution)/shard_map/reshape | solution.py:43
  127.6 2.7 %fusion = bf16[20,4,256]{2,0,1:T(8,128)(2,1)S(1)} fusion(f32[4,96,256]{2,1,0:T(8,128)S(1)} %copy.59, bf16[20,4,96,96]{3,2,1,0:T(8,128)(2,1)} %reshape.46, bf16[4,96,256,1]{2,0,1,3:T(4,128)(2,1)S(1)} %copy-done.8), kind=kOutput, calls=%fused_computation.3 | convolution fusion | flops 381399040 | bytes 2105344 | tf_op jit(solution)/shard_map/iomx,oxj->iomj/dot_general | solution.py:44
  130.4 9.5 %all_gather.12 = bf16[80,2048]{1,0:T(8,128)(2,1)S(1)} all-gather(bf16[80,256]{1,0:T(8,128)(2,1)S(1)} %convert_element_type.102), channel_id=1, replica_groups=mesh['pb'=4,'row'=4,'col'=2] {'row','col'}, dimensions={1}, use_global_device_ids=true | all-gather | bytes 368640 | tf_op jit(solution)/shard_map/all_gather | solution.py:52
  139.8 1.1 convolution_convert_fusion.2
  140.9 0.0 reduce-scatter.5.cloned.1.call-update
  140.9 0.2 all-reduce.5.cloned.1.call-start
  141.2 7.4 %reduce-scatter.5.cloned.1.call-done = bf16[80,256]{1,0:T(8,128)(2,1)} async-done(((bf16[80,512]{1,0:T(8,128)(2,1)}), bf16[80,256]{1,0:T(8,128)(2,1)}) %reduce-scatter.5.cloned.1.call-update) | async-done | bytes 40976 | tf_op jit(solution)/shard_map/reduce_scatter | solution.py:58
  148.6 0.8 reshape.50
  149.4 2.9 %convert_bitcast_fusion = bf16[20,4,96,96]{2,3,0,1:T(8,128)(2,1)} fusion(f32[20,4,256]{2,0,1:T(8,128)S(1)} %copy.69, f32[4,96,256]{2,1,0:T(8,128)S(1)} %copy.59, bf16[4,96,256,1]{2,0,1,3:T(4,128)(2,1)S(1)} %copy-done.8), kind=kOutput, calls=%fused_computation.24 | convolution fusion | flops 382156800 | bytes 2146304 | tf_op jit(solution)/shard_map/kyqz,yhz->kyqh/dot_general | solution.py:67
  152.3 3.2 %copy.71 = bf16[20,4,96,96]{3,2,1,0:T(8,128)(2,1)S(1)} copy(bf16[20,4,96,96]{2,3,0,1:T(8,128)(2,1)} %convert_bitcast_fusion) | data formatting | bytes 2949120 | tf_op jit(solution)/shard_map/convert_element_type | solution.py:82
  155.5 3.6 %convert_element_type.107 = bf16[80,9216]{1,0:T(8,128)(2,1)} reshape(bf16[20,4,96,96]{3,2,1,0:T(8,128)(2,1)S(1)} %copy.71) | data formatting | bytes 2949120 | tf_op jit(solution)/shard_map/convert_element_type | solution.py:82
  159.1 0.0 all-reduce.5.cloned.1.call-update
  159.1 59.7 %all-reduce.5.cloned.1.call-done = bf16[80,9216]{1,0:T(8,128)(2,1)} async-done(((bf16[80,9216]{1,0:T(8,128)(2,1)}), bf16[80,9216]{1,0:T(8,128)(2,1)}) %all-reduce.5.cloned.1.call-update) | async-done | bytes 1474576 | tf_op jit(solution)/shard_map/psum | solution.py:82
  218.8 4.8 %fusion.12 = bf16[80,9216]{1,0:T(8,128)(2,1)S(1)} fusion(f32[80,9216]{1,0:T(8,128)} %reshape.48, f32[80,9216]{1,0:T(8,128)} %tile.9, bf16[80,9216]{1,0:T(8,128)(2,1)} %all-reduce.5.cloned.1.call-done, bf16[80,9216]{1,0:T(8,128)(2,1)} %all-reduce.3.cloned.1.call-done), kind=kLoop, calls=%fused_computation.20 | loop fusion | flops 11796480 | bytes 10321920 | tf_op jit(solution)/shard_map/convert_element_type | solution.py:79
  223.6 1.4 reshape.47
  (24 shorter events, 0.2 us)
Async XLA Ops:
  6.5 34.5 %copy-start = (bf16[1,512,1024]{2,1,0:T(8,128)(2,1)S(1)}, bf16[1,512,1024]{2,1,0:T(8,128)(2,1)}, u32[]{:S(2)}) copy-start(bf16[1,512,1024]{2,1,0:T(8,128)(2,1)} %param.15) | copy-start | bytes 3145732
  6.5 18.5 %copy-start.1 = (bf16[1,20,4,9216]{3,2,1,0:T(4,128)(2,1)S(1)}, bf16[1,20,4,9216]{3,2,1,0:T(4,128)(2,1)}, u32[]{:S(2)}) copy-start(bf16[1,20,4,9216]{3,2,1,0:T(4,128)(2,1)} %param.9) | copy-start | bytes 4423684
  6.5 44.1 %reduce-scatter.3.cloned.1.call-start = ((), (), s32[]{:S(2)}) async-start(), calls=%async_computation.2 | async-start | bytes 122880 | tf_op jit(solution)/shard_map/reduce_scatter | solution.py:58
  7.4 20.3 %copy-start.5 = (s32[4]{0:T(128)S(1)}, s32[4]{0:T(128)}, u32[]{:S(2)}) copy-start(s32[4]{0:T(128)} %param.11) | copy-start | bytes 52
  28.0 2.8 %copy-start.6 = (bf16[4,96,256,1]{2,0,1,3:T(4,128)(2,1)}, bf16[4,96,256,1]{2,0,1,3:T(4,128)(2,1)S(1)}, u32[]{:S(2)}) copy-start(bf16[4,96,256,1]{2,0,1,3:T(4,128)(2,1)S(1)} %fusion.16) | copy-start | bytes 589828
  41.0 2.9 %copy-start.4 = (s32[1,4,2]{1,2,0:T(2,128)S(1)}, s32[1,4,2]{1,2,0:T(2,128)}, u32[]{:S(2)}) copy-start(s32[1,4,2]{1,2,0:T(2,128)} %param.10) | copy-start | bytes 100
  42.1 9.3 %copy-start.7 = (bf16[4,96,256,1]{2,0,1,3:T(4,128)(2,1)S(1)}, bf16[4,96,256,1]{2,0,1,3:T(4,128)(2,1)}, u32[]{:S(2)}) copy-start(bf16[4,96,256,1]{2,0,1,3:T(4,128)(2,1)} %copy-done.6) | copy-start | bytes 589828
  42.1 78.7 %all-reduce.3.cloned.1.call-start = ((), (), s32[]{:S(2)}) async-start(), calls=%async_computation.3 | async-start | bytes 2949120 | tf_op jit(solution)/shard_map/psum | solution.py:82
  57.5 3.7 %copy-start.2 = (f32[4,96]{1,0:T(4,128)S(1)}, f32[4,96]{1,0:T(4,128)}, u32[]{:S(2)}) copy-start(f32[4,96]{1,0:T(4,128)} %param.13) | copy-start | bytes 4612
  57.5 4.2 %copy-start.3 = (f32[4,96]{1,0:T(4,128)S(1)}, f32[4,96]{1,0:T(4,128)}, u32[]{:S(2)}) copy-start(f32[4,96]{1,0:T(4,128)} %param.14) | copy-start | bytes 4612
  61.1 87.5 %reduce-scatter.5.cloned.1.call-start = ((), (), s32[]{:S(2)}) async-start(), calls=%async_computation.4 | async-start | bytes 122880 | tf_op jit(solution)/shard_map/reduce_scatter | solution.py:58
  124.6 2.9 %copy-start.8 = (bf16[4,96,256,1]{2,0,1,3:T(4,128)(2,1)S(1)}, bf16[4,96,256,1]{2,0,1,3:T(4,128)(2,1)}, u32[]{:S(2)}) copy-start(bf16[4,96,256,1]{2,0,1,3:T(4,128)(2,1)} %copy-done.6) | copy-start | bytes 589828
  140.9 77.9 %all-reduce.5.cloned.1.call-start = ((), (), s32[]{:S(2)}) async-start(), calls=%async_computation.5 | async-start | bytes 2949120 | tf_op jit(solution)/shard_map/psum | solution.py:82
Sparse Core Ops, SparseCore 0:
  42.2 8.3 reduce-scatter.2
  61.3 59.5 all-reduce.2
  141.1 7.5 reduce-scatter.4
  159.2 59.5 all-reduce.4
where the time goes:
time: 232 us
  waiting for transfers between devices  125 us (54%)
  blocking collectives  36.2 us (16%)
  local copies, waits for them, and re-layouts  32.7 us (14%)
  matrix products  14.8 us (6%)
  between operations  13.3 us (6%)
  other arithmetic  8.91 us (4%)
    psum x2, waiting for transfers between devices, finish(): lax.psum(partial_term.astype(jnp.bfloat16), ('row', 'col'))  111 us
    all_gather x2, blocking collectives, kernel_term(): everywhere = lax.all_gather(values, ('row', 'col'), axis=1, tiled=True)  19.6 us
    all_gather x1, blocking collectives, fetch_each(): found = pick(lax.all_gather(orbitals, 'pb', axis=0, tiled=True))  16.6 us
    reduce_scatter x2, waiting for transfers between devices, kernel_term(): lax.psum_scatter(partial_value.astype(jnp.bfloat16), 'col', scatter_dimen...  14.1 us
    convert_element_type x4, local copies, waits for them, and re-layouts, finish(): partial_term.astype(jnp.bfloat16)  13.5 us
    another operation x2, local copies, waits for them, and re-layouts, on_device(): gap_rows = jnp.tile(gap_grid, (vectors, 1))  6.56 us
    dot_general x2, matrix products, kernel_term(): jnp.einsum('kyqz,yhz->kyqh', weighted_product, conduction_orbital, prefer...  5.75 us
    dot_general x2, matrix products, kernel_term(): jnp.einsum('iomx,oxj->iomj', amplitude_lattice, conduction_orbital, prefe...  5.54 us
  transfers between devices with their start and end apart: 4, of which 4 were waited for; matrix products, arithmetic and copies ran while one was open for 4% of the time, Pallas kernels for 0%

commit v1 on v0

--- a/solution.py
+++ b/solution.py
@@ -79,7 +79,9 @@
         return (factor * value - previous_rows).astype(jnp.bfloat16)
 
     def finish(partial_term, current, previous, factor):
-        summed = lax.psum(partial_term.astype(jnp.bfloat16), ("row", "col")).astype(jnp.float32)
+        summed = lax.psum(lax.psum(partial_term.astype(jnp.bfloat16), "col"), "row").astype(
+            jnp.float32
+        )
         previous_full = None
         if previous is not None:
             previous_full = previous.astype(jnp.float32)

time: 232 us -> 287 us (1.24)
  waiting for transfers between devices: 125 us -> 176 us
    psum x2 -> x4, waiting for transfers between devices: 111 us -> 160 us  [the longest x2 117 us: finish(): lax.psum(lax.psum(partial_term.astype(jnp.bfloat16), 'col'), 'row')]
  transfers between devices with their start and end apart: 4 -> 6, of which waited for: 4 -> 6; matrix products, arithmetic and copies ran while one was open for 4% -> 3% of each run, Pallas kernels for 0% -> 0%
where the time goes in v1:
time: 287 us; the launch traced here: 286 us
  waiting for transfers between devices  176 us (61%)
  blocking collectives  36.8 us (13%)
  local copies, waits for them, and re-layouts  34.9 us (12%)
  matrix products  14.8 us (5%)
  between operations  13.7 us (5%)
  other arithmetic  9.7 us (3%)
    psum x2, waiting for transfers between devices, finish(): lax.psum(lax.psum(partial_term.astype(jnp.bfloat16), 'col'), 'row')  117 us
    psum x2, waiting for transfers between devices, finish(): lax.psum(partial_term.astype(jnp.bfloat16), 'col')  42.8 us
    all_gather x2, blocking collectives, kernel_term(): everywhere = lax.all_gather(values, ('row', 'col'), axis=1, tiled=True)  20.2 us
    all_gather x1, blocking collectives, fetch_each(): found = pick(lax.all_gather(orbitals, 'pb', axis=0, tiled=True))  16.6 us
    reduce_scatter x2, waiting for transfers between devices, kernel_term(): lax.psum_scatter(partial_value.astype(jnp.bfloat16), 'col', scatter_dimen...  15.9 us
    convert_element_type x4, local copies, waits for them, and re-layouts, finish(): partial_term.astype(jnp.bfloat16)  13.5 us
    another operation x2, local copies, waits for them, and re-layouts, on_device(): gap_rows = jnp.tile(gap_grid, (vectors, 1))  6.53 us
    dot_general x2, matrix products, kernel_term(): jnp.einsum('kyqz,yhz->kyqh', weighted_product, conduction_orbital, prefer...  5.76 us
  transfers between devices with their start and end apart: 6, of which 6 were waited for; matrix products, arithmetic and copies ran while one was open for 3% of the time, Pallas kernels for 0%

profile of v1, /device:TPU:0, one launch (start us, length us, event | category | flops | bytes accessed | tf_op | source)
XLA Modules:
  0.0 286.2 jit_solution(8528285945165947028)
XLA Ops:
  6.5 0.8 slice_bitcast_fusion.1
  7.4 16.6 %all_gather.10 = bf16[4,192,256]{2,1,0:T(8,128)(2,1)S(1)} all-gather(bf16[1,192,256]{2,1,0:T(8,128)(2,1)} %param.12), channel_id=1, replica_groups=mesh['pb'=4,'row'=4,'col'=2] {'pb'}, dimensions={0}, use_global_device_ids=true | all-gather | bytes 491520 | tf_op jit(solution)/shard_map/all_gather | solution.py:33
  24.0 1.0 fusion.15
  25.0 0.1 copy.59
  25.1 2.6 reshape_reshape_squeeze.3
  27.7 0.3 fusion.16
  28.0 2.8 fusion.1
  30.9 10.1 %all_gather.11 = bf16[80,2048]{1,0:T(8,128)(2,1)S(1)} all-gather(bf16[80,256]{1,0:T(8,128)(2,1)S(1)} %convert_element_type.92), channel_id=1, replica_groups=mesh['pb'=4,'row'=4,'col'=2] {'row','col'}, dimensions={1}, use_global_device_ids=true | all-gather | bytes 368640 | tf_op jit(solution)/shard_map/all_gather | solution.py:52
  41.0 1.1 convolution_convert_fusion.3
  42.1 0.0 reduce-scatter.3.cloned.1.call-update
  42.1 0.0 all-reduce.5.cloned.1.call-start
  42.1 8.4 %reduce-scatter.3.cloned.1.call-done = bf16[80,256]{1,0:T(8,128)(2,1)} async-done(((bf16[80,512]{1,0:T(8,128)(2,1)}), bf16[80,256]{1,0:T(8,128)(2,1)}) %reduce-scatter.3.cloned.1.call-update) | async-done | bytes 40976 | tf_op jit(solution)/shard_map/reduce_scatter | solution.py:58
  50.6 0.8 reshape.49
  51.4 2.9 %convert_bitcast_fusion.1 = bf16[20,4,96,96]{2,3,0,1:T(8,128)(2,1)} fusion(f32[20,4,256]{2,0,1:T(8,128)S(1)} %copy.63, f32[4,96,256]{2,1,0:T(8,128)S(1)} %copy.59, bf16[4,96,256,1]{2,0,1,3:T(4,128)(2,1)S(1)} %fusion.16), kind=kOutput, calls=%fused_computation.25 | convolution fusion | flops 382156800 | bytes 2146304 | tf_op jit(solution)/shard_map/kyqz,yhz->kyqh/dot_general | solution.py:67
  54.3 3.2 %copy.65 = bf16[20,4,96,96]{3,2,1,0:T(8,128)(2,1)S(1)} copy(bf16[20,4,96,96]{2,3,0,1:T(8,128)(2,1)} %convert_bitcast_fusion.1) | data formatting | bytes 2949120 | tf_op jit(solution)/shard_map/convert_element_type | solution.py:82
  57.5 3.6 %convert_element_type.97 = bf16[80,9216]{1,0:T(8,128)(2,1)} reshape(bf16[20,4,96,96]{3,2,1,0:T(8,128)(2,1)S(1)} %copy.65) | data formatting | bytes 2949120 | tf_op jit(solution)/shard_map/convert_element_type | solution.py:82
  61.1 0.0 all-reduce.5.cloned.1.call-update
  61.1 0.0 all-reduce.7.cloned.1.call-start
  61.1 21.4 %all-reduce.5.cloned.1.call-done = bf16[80,9216]{1,0:T(8,128)(2,1)} async-done(((bf16[80,9216]{1,0:T(8,128)(2,1)}), bf16[80,9216]{1,0:T(8,128)(2,1)}) %all-reduce.5.cloned.1.call-update) | async-done | bytes 1474576 | tf_op jit(solution)/shard_map/psum | solution.py:82
  82.6 0.0 all-reduce.7.cloned.1.call-update
  82.6 0.0 reduce-scatter.5.cloned.1.call-start
  82.7 1.7 reshape.48
  84.4 0.6 gather_fusion.1
  85.0 0.6 gather_fusion
  85.5 0.1 broadcast_select_fusion
  85.6 0.1 broadcast_select_fusion.1
  85.7 0.1 broadcast_subtract_fusion
  85.8 0.2 sub.32
  86.0 2.3 tile.8
  88.3 4.3 %tile.9 = f32[80,9216]{1,0:T(8,128)} reshape(f32[20,4,9216]{2,1,0:T(4,128)} %tile.8) | data formatting | bytes 5898240 | tf_op jit(solution)/shard_map/tile | solution.py:39
  92.5 53.7 %all-reduce.7.cloned.1.call-done = bf16[80,9216]{1,0:T(8,128)(2,1)} async-done(((bf16[80,9216]{1,0:T(8,128)(2,1)}), bf16[80,9216]{1,0:T(8,128)(2,1)}) %all-reduce.7.cloned.1.call-update) | async-done | bytes 1474576 | tf_op jit(solution)/shard_map/psum | solution.py:82
  146.2 3.8 %multiply_convert_fusion.4 = bf16[80,9216]{1,0:T(8,128)(2,1)S(1)} fusion(f32[80,9216]{1,0:T(8,128)} %reshape.48, bf16[80,9216]{1,0:T(8,128)(2,1)} %all-reduce.7.cloned.1.call-done, f32[80,9216]{1,0:T(8,128)} %tile.9), kind=kLoop, calls=%fused_computation.21 | loop fusion | flops 5160960 | bytes 8847360 | tf_op jit(solution)/shard_map/convert_element_type | solution.py:78
  150.0 2.9 %reshape.46 = bf16[20,4,96,96]{3,2,1,0:T(8,128)(2,1)} reshape(bf16[80,9216]{1,0:T(8,128)(2,1)S(1)} %multiply_convert_fusion.4) | data formatting | bytes 2949120 | tf_op jit(solution)/shard_map/reshape | solution.py:43
  152.9 2.7 fusion
  155.7 10.1 %all_gather.12 = bf16[80,2048]{1,0:T(8,128)(2,1)S(1)} all-gather(bf16[80,256]{1,0:T(8,128)(2,1)S(1)} %convert_element_type.102), channel_id=1, replica_groups=mesh['pb'=4,'row'=4,'col'=2] {'row','col'}, dimensions={1}, use_global_device_ids=true | all-gather | bytes 368640 | tf_op jit(solution)/shard_map/all_gather | solution.py:52
  165.8 1.1 convolution_convert_fusion.2
  166.9 0.2 all-reduce.9.cloned.1.call-start
  167.1 7.5 %reduce-scatter.5.cloned.1.call-done = bf16[80,256]{1,0:T(8,128)(2,1)} async-done(((bf16[80,512]{1,0:T(8,128)(2,1)}), bf16[80,256]{1,0:T(8,128)(2,1)}) %reduce-scatter.5.cloned.1.call-update) | async-done | bytes 40976 | tf_op jit(solution)/shard_map/reduce_scatter | solution.py:58
  174.6 0.8 reshape.50
  175.4 2.9 convert_bitcast_fusion
  178.3 3.2 %copy.71 = bf16[20,4,96,96]{3,2,1,0:T(8,128)(2,1)S(1)} copy(bf16[20,4,96,96]{2,3,0,1:T(8,128)(2,1)} %convert_bitcast_fusion) | data formatting | bytes 2949120 | tf_op jit(solution)/shard_map/convert_element_type | solution.py:82
  181.5 3.6 %convert_element_type.107 = bf16[80,9216]{1,0:T(8,128)(2,1)} reshape(bf16[20,4,96,96]{3,2,1,0:T(8,128)(2,1)S(1)} %copy.71) | data formatting | bytes 2949120 | tf_op jit(solution)/shard_map/convert_element_type | solution.py:82
  185.1 0.0 all-reduce.9.cloned.1.call-update
  185.1 0.0 all-reduce.11.cloned.1.call-start
  185.1 21.4 %all-reduce.9.cloned.1.call-done = bf16[80,9216]{1,0:T(8,128)(2,1)} async-done(((bf16[80,9216]{1,0:T(8,128)(2,1)}), bf16[80,9216]{1,0:T(8,128)(2,1)}) %all-reduce.9.cloned.1.call-update) | async-done | bytes 1474576 | tf_op jit(solution)/shard_map/psum | solution.py:82
  206.6 63.5 %all-reduce.11.cloned.1.call-done = bf16[80,9216]{1,0:T(8,128)(2,1)} async-done(((bf16[80,9216]{1,0:T(8,128)(2,1)}), bf16[80,9216]{1,0:T(8,128)(2,1)}) %all-reduce.11.cloned.1.call-update) | async-done | bytes 1474576 | tf_op jit(solution)/shard_map/psum | solution.py:82
  270.0 5.6 %fusion.12 = bf16[80,9216]{1,0:T(8,128)(2,1)} fusion(f32[80,9216]{1,0:T(8,128)} %reshape.48, f32[80,9216]{1,0:T(8,128)} %tile.9, bf16[80,9216]{1,0:T(8,128)(2,1)} %all-reduce.11.cloned.1.call-done, bf16[80,9216]{1,0:T(8,128)(2,1)S(1)} %copy-done.1), kind=kLoop, calls=%fused_computation.20 | loop fusion | flops 11796480 | bytes 10321920 | tf_op jit(solution)/shard_map/convert_element_type | solution.py:79
  275.7 3.6 %reshape.47 = bf16[1,20,4,9216]{3,2,1,0:T(4,128)(2,1)} reshape(bf16[80,9216]{1,0:T(8,128)(2,1)} %fusion.12) | data formatting | bytes 2949120 | tf_op jit(solution)/shard_map/reshape | solution.py:95
  (32 shorter events, 0.2 us)
Async XLA Ops:
  6.5 34.4 %copy-start = (bf16[1,512,1024]{2,1,0:T(8,128)(2,1)S(1)}, bf16[1,512,1024]{2,1,0:T(8,128)(2,1)}, u32[]{:S(2)}) copy-start(bf16[1,512,1024]{2,1,0:T(8,128)(2,1)} %param.15) | copy-start | bytes 3145732
  6.5 18.5 %copy-start.2 = (bf16[1,20,4,9216]{3,2,1,0:T(4,128)(2,1)S(1)}, bf16[1,20,4,9216]{3,2,1,0:T(4,128)(2,1)}, u32[]{:S(2)}) copy-start(bf16[1,20,4,9216]{3,2,1,0:T(4,128)(2,1)} %param.9) | copy-start | bytes 4423684
  6.5 44.0 %reduce-scatter.3.cloned.1.call-start = ((), (), s32[]{:S(2)}) async-start(), calls=%async_computation.2 | async-start | bytes 122880 | tf_op jit(solution)/shard_map/reduce_scatter | solution.py:58
  7.4 20.3 %copy-start.7 = (s32[4]{0:T(128)S(1)}, s32[4]{0:T(128)}, u32[]{:S(2)}) copy-start(s32[4]{0:T(128)} %param.11) | copy-start | bytes 52
  28.0 23.4 %copy-start.8 = (bf16[4,96,256,1]{2,0,1,3:T(4,128)(2,1)}, bf16[4,96,256,1]{2,0,1,3:T(4,128)(2,1)S(1)}, u32[]{:S(2)}) copy-start(bf16[4,96,256,1]{2,0,1,3:T(4,128)(2,1)S(1)} %fusion.16) | copy-start | bytes 589828
  42.1 40.5 %all-reduce.5.cloned.1.call-start = ((), (), s32[]{:S(2)}) async-start(), calls=%async_computation.3 | async-start | bytes 2949120 | tf_op jit(solution)/shard_map/psum | solution.py:82
  61.1 21.6 %copy-start.3 = (bf16[1,20,4,9216]{3,2,1,0:T(4,128)(2,1)S(1)}, bf16[1,20,4,9216]{3,2,1,0:T(4,128)(2,1)}, u32[]{:S(2)}) copy-start(bf16[1,20,4,9216]{3,2,1,0:T(4,128)(2,1)} %param.9) | copy-start | bytes 4423684
  61.1 85.1 %all-reduce.7.cloned.1.call-start = ((), (), s32[]{:S(2)}) async-start(), calls=%async_computation.4 | async-start | bytes 2949120 | tf_op jit(solution)/shard_map/psum | solution.py:82
  82.6 1.8 copy-start.6
  82.6 1.8 copy-start.4
  82.6 2.4 copy-start.5
  82.6 92.0 %reduce-scatter.5.cloned.1.call-start = ((), (), s32[]{:S(2)}) async-start(), calls=%async_computation.5 | async-start | bytes 122880 | tf_op jit(solution)/shard_map/reduce_scatter | solution.py:58
  150.0 2.9 %copy-start.9 = (bf16[4,96,256,1]{2,0,1,3:T(4,128)(2,1)S(1)}, bf16[4,96,256,1]{2,0,1,3:T(4,128)(2,1)}, u32[]{:S(2)}) copy-start(bf16[4,96,256,1]{2,0,1,3:T(4,128)(2,1)} %copy-done.8) | copy-start | bytes 589828
  166.9 39.6 %all-reduce.9.cloned.1.call-start = ((), (), s32[]{:S(2)}) async-start(), calls=%async_computation.6 | async-start | bytes 2949120 | tf_op jit(solution)/shard_map/psum | solution.py:82
  185.1 85.0 %copy-start.1 = (bf16[80,9216]{1,0:T(8,128)(2,1)S(1)}, bf16[80,9216]{1,0:T(8,128)(2,1)}, u32[]{:S(2)}) copy-start(bf16[80,9216]{1,0:T(8,128)(2,1)} %all-reduce.7.cloned.1.call-done) | copy-start | bytes 4423684
  185.1 85.0 %all-reduce.11.cloned.1.call-start = ((), (), s32[]{:S(2)}) async-start(), calls=%async_computation.7 | async-start | bytes 2949120 | tf_op jit(solution)/shard_map/psum | solution.py:82
Sparse Core Ops, SparseCore 0:
  42.2 8.3 reduce-scatter.2
  61.2 21.3 all-reduce.4
  85.7 60.4 all-reduce.6
  167.0 7.5 reduce-scatter.4
  185.2 21.3 all-reduce.8
  209.6 60.4 all-reduce.10
